TPU v7x, 128 devices: a whole 4x4x4 slice. The times are simulated.
128 devices in a mesh: seq: 128 (over z, x, y, core).
Axes of the slice: x: 4, y: 4, z: 4, core: 2. Of those that a mesh axis runs over, the one named last changes fastest.
Arguments:
- tokens: bfloat16 [65536, 1024], P('seq'), may hold values from -6 to 6
- init_state: bfloat16 [512, 1024], replicated, may hold values from -6 to 6
- w_query: bfloat16 [1024, 1024], replicated, may hold values from -1 to 1
- w_key: bfloat16 [1024, 1024], replicated, may hold values from -1 to 1
- w_value: bfloat16 [1024, 1024], replicated, may hold values from -0.1875 to 0.1875
- w_out: bfloat16 [1024, 1024], replicated, may hold values from -0.1875 to 0.1875
- w_query_state: bfloat16 [1024, 1024], replicated, may hold values from -1 to 1
- w_cand_gate: bfloat16 [1024, 2048], replicated, may hold values from -0.1875 to 0.1875
- w_state_kv: bfloat16 [1024, 2048], replicated, may hold values from -0.1875 to 0.1875
- gate_bias: float32 [1024], replicated, may hold values from -2 to 5
- mixing: float32 [2, 3], replicated, may hold values from 0.2 to 0.6
- retrieval: int32 [128, 8], P('seq'), may hold values from 0 to 31, all different within a row
Outputs:
- mixed: bfloat16 [65536, 1024], P('seq')
- new_state: bfloat16 [65536, 1024], P('seq')
Inputs may be any that keep to these rules, and one draw needn't show every extreme that they name: `retrieval`: entries of one segment differ. Entry e names block e % 8 of the segment e // 8 + 1 places earlier; entries reaching before the first segment are ignored.
All inputs are finite; a program needn't handle non-finite values.
Results may differ from a plain program's by a relative error of at most 0.008.
Values may be sent and summed in bfloat16 or wider, within the bound.
A program may use at most 128 MiB of HBM per device.

v0:
```python
import jax
import jax.numpy as jnp
from jax import lax
from jax.experimental import pallas as pl
from jax.experimental.pallas import tpu as pltpu
from jax.sharding import PartitionSpec as P

HEADS = 8
HW = 128
D = 1024
SEG = 512
BLK = 64
RET = 8
ITERS = 2
ROWS = 256
CHUNKS = SEG // ROWS
HALF = RET // 2
LOG2E = 1.4426950408889634
SCALE = LOG2E / HW**0.5
NEG = -1e30
F32 = jnp.float32
BF16 = jnp.bfloat16
MESH = pl.DeviceIdType.MESH


def dot(a, b):
    return jnp.dot(a, b, preferred_element_type=F32)


def dot_nt(a, b):
    return lax.dot_general(a, b, (((1,), (1,)), ((), ())), preferred_element_type=F32)


def rows_of(chunk):
    return pl.ds(pl.multiple_of(chunk * ROWS, ROWS), ROWS)


def project(dst, src, weight, columns, step=512):
    def body(n, carry):
        cols = pl.ds(pl.multiple_of(n * step, step), step)
        dst[:, cols] = dot(src[...], weight[:, cols]).astype(BF16)
        return carry

    lax.fori_loop(0, columns // step, body, 0)


def with_ones(v):
    return jnp.concatenate([v, jnp.ones((v.shape[0], HW), BF16)], axis=1)


def self_attention(query, keys, values, out):
    for h in range(HEADS):
        cols = slice(h * HW, (h + 1) * HW)
        s = dot_nt(query[:, cols], keys[:, cols])
        m = jnp.max(s, axis=1, keepdims=True) * SCALE
        p = jnp.exp2(s * SCALE - m).astype(BF16)
        ol = dot(p, with_ones(values[:, cols]))
        out[:, cols] = (ol[:, :HW] / ol[:, HW:]).astype(BF16)


def partial_attention(query, keys, values, acc, peak, mask, first, out):
    count = query.shape[0]
    for h in range(HEADS):
        cols = slice(h * HW, (h + 1) * HW)
        wide = slice(h * 2 * HW, (h + 1) * 2 * HW)
        s = dot_nt(query[:, cols], keys[:, cols]) * SCALE
        if mask is not None:
            s = jnp.where(mask, s, NEG)
        m = jnp.broadcast_to(jnp.max(s, axis=1, keepdims=True), (count, HW))
        if not first:
            old = peak[:, cols]
            m = jnp.maximum(m, old)
        p = jnp.exp2(s - jnp.concatenate([m] * (s.shape[1] // HW), axis=1)).astype(BF16)
        ol = dot(p, with_ones(values[:, cols]))
        if not first:
            alpha = jnp.exp2(old - m)
            ol = ol + jnp.concatenate([alpha, alpha], axis=1) * acc[:, wide]
        if out is None:
            acc[:, wide] = ol
            peak[:, cols] = m
        else:
            out[:, cols] = (ol[:, :HW] / ol[:, HW:]).astype(BF16)


def gate(attended, weight, bias, state, out, step=512):
    def body(n, carry):
        left = pl.ds(pl.multiple_of(n * step, step), step)
        right = pl.ds(pl.multiple_of(D + n * step, step), step)
        cand = jnp.tanh(dot(attended[...], weight[:, left]))
        forget = 0.5 + 0.5 * jnp.tanh(0.5 * (dot(attended[...], weight[:, right]) + bias[:, left]))
        out[:, left] = (cand + forget * (state[:, left].astype(F32) - cand)).astype(BF16)
        return carry

    lax.fori_loop(0, D // step, body, 0)


def make_kernel(count, comm):
    def kernel(
        tokens, tokens_flat, init, wq, wk, wv, wo, wqs, wcg, wskv, bias, mixing, retrieval,
        mixed, new_state,
        buf, own, relay, vq, vk, vv, vo, vqs, vcg, vskv,
        key, value, mkey, mvalue, skv, qtok, xmem,
        state0, guess, outs, shifted, query, att, final, acc, peak,
        load_sem, out_sem, send_sem, recv_sem,
    ):
        me = lax.axis_index("seq") if comm else jnp.int32(7)
        core = me % 2

        def wrap(index):
            return (index + count) % count

        def minus_y(index):
            return index // 8 * 8 + (index // 2 + 3) % 4 * 2 + index % 2

        def plus_y(index):
            return index // 8 * 8 + (index // 2 + 1) % 4 * 2 + index % 2

        sibling = me + 1 - 2 * core
        nxt, prev = wrap(me + 1), wrap(me - 1)
        two_on, two_back = wrap(me + 2), wrap(me - 2)
        relay_to, relay_from = minus_y(me), plus_y(me)
        final_to = wrap(relay_from + 4)
        final_from = minus_y(wrap(me - 4))

        loads = {}

        def load(name, n, src, dst):
            loads[name] = pltpu.make_async_copy(src, dst, load_sem.at[n])
            loads[name].start()

        load("tokens", 0, tokens, buf.at[pl.ds(0, RET)])
        load("own", 9, tokens_flat, own)
        load("wk", 1, wk, vk)
        load("wv", 2, wv, vv)
        load("init", 3, init, state0)
        load("wqs", 4, wqs, vqs)
        load("wcg", 5, wcg, vcg)
        load("wq", 6, wq, vq)
        load("wskv", 7, wskv, vskv)
        load("wo", 8, wo, vo)

        def remote(n, src, dst, device):
            return pltpu.make_async_remote_copy(
                src_ref=src, dst_ref=dst, send_sem=send_sem.at[n], recv_sem=recv_sem.at[n],
                device_id=(device,), device_id_type=MESH,
            )

        def slot(d, half=None):
            if half is None:
                return buf.at[pl.ds(d * RET, RET)]
            return buf.at[pl.ds(d * RET + half * HALF, HALF)]

        hop = remote(0, slot(0), slot(2), two_on)
        to_relay = [remote(1 + k, slot(0, k), relay.at[pl.ds(k * HALF, HALF)], relay_to) for k in range(2)]
        from_relay = [remote(3 + k, relay.at[pl.ds(k * HALF, HALF)], slot(4, k), final_to) for k in range(2)]
        near = remote(5, buf.at[pl.ds(core * 2 * RET, RET)], slot(1), sibling)
        far = remote(6, buf.at[pl.ds((core + 1) * 2 * RET, RET)], slot(3), sibling)

        def state_copy(sweep, chunk):
            return remote(
                7 + sweep * CHUNKS + chunk, outs.at[sweep, rows_of(chunk)],
                shifted.at[sweep, rows_of(chunk)], nxt,
            )

        if comm:
            barrier = pltpu.get_barrier_semaphore()
            for source in (sibling, prev, two_back, relay_from, final_from):
                pl.semaphore_signal(barrier, inc=1, device_id=(source,), device_id_type=MESH)
            pl.semaphore_wait(barrier, 5)
        loads["tokens"].wait()
        if comm:
            to_relay[0].start()
            to_relay[1].start()

            @pl.when(core == 0)
            def _():
                hop.start()
                near.start()

        loads["own"].wait()
        loads["wk"].wait()
        project(key, own, vk, D)
        loads["wv"].wait()
        project(value, own, vv, D)
        loads["init"].wait()
        loads["wqs"].wait()

        first_segment = me == 0

        def forward_state(sweep):
            source = state0 if sweep == 0 else guess

            def chunk_body(chunk, carry):
                rows = rows_of(chunk)
                if sweep > 0:
                    if comm:
                        state_copy(sweep - 1, chunk).wait_recv()
                    base = state0[rows].astype(F32)
                    moved = jnp.where(first_segment, base, shifted[sweep - 1, rows].astype(F32))
                    if sweep == 1:
                        held, older = base, base
                    else:
                        held = guess[rows].astype(F32)
                        older = jnp.where(first_segment, base, shifted[sweep - 2, rows].astype(F32))
                    guess[rows] = (
                        mixing[sweep - 1, 0] * moved + mixing[sweep - 1, 1] * held + mixing[sweep - 1, 2] * older
                    ).astype(BF16)
                project(query.at[rows], source.at[rows], vqs, D)
                if sweep < ITERS and comm:
                    @pl.when(chunk > 0)
                    def _():
                        state_copy(sweep, chunk - 1).start()
                self_attention(query.at[rows], key, value, att.at[rows])
                if sweep == 0:
                    @pl.when(chunk == 0)
                    def _():
                        loads["wcg"].wait()
                gate(att.at[rows], vcg, bias, source.at[rows], (outs.at[sweep] if sweep < ITERS else final).at[rows])
                return carry

            lax.fori_loop(0, CHUNKS, chunk_body, 0)

        def last_send(sweep):
            if comm:
                state_copy(sweep, CHUNKS - 1).start()

        def local_attention(chunk):
            rows = slice(chunk * ROWS, (chunk + 1) * ROWS)
            width = (chunk + 1) * ROWS
            row = lax.broadcasted_iota(jnp.int32, (ROWS, width), 0) + chunk * ROWS
            col = lax.broadcasted_iota(jnp.int32, (ROWS, width), 1)
            partial_attention(
                qtok.at[rows], key.at[slice(0, width)], value.at[slice(0, width)],
                acc.at[rows], peak.at[rows], col <= row, True, None,
            )

        forward_state(0)
        loads["wq"].wait()
        project(qtok, own, vq, D)
        last_send(0)
        if comm:
            to_relay[0].wait_recv()
            from_relay[0].start()
        local_attention(0)
        forward_state(1)
        if comm:
            to_relay[1].wait_recv()
            from_relay[1].start()
        local_attention(1)
        last_send(1)
        if comm:
            @pl.when(core == 1)
            def _():
                hop.start()

            @pl.when(core == 0)
            def _():
                hop.wait_recv()
                far.start()
        forward_state(2)
        store_state = pltpu.make_async_copy(final, new_state, out_sem.at[0])
        loads["wskv"].wait()
        project(skv, guess, vskv, 2 * D)
        store_state.start()

        def state_part(chunk, carry):
            rows = rows_of(chunk)
            partial_attention(
                qtok.at[rows], skv.at[:, pl.ds(0, D)], skv.at[:, pl.ds(D, D)],
                acc.at[rows], peak.at[rows], None, False, None,
            )
            return carry

        lax.fori_loop(0, CHUNKS, state_part, 0)

        if comm:
            @pl.when(core == 1)
            def _():
                hop.wait_recv()
                near.start()
                from_relay[0].wait_recv()
                from_relay[1].wait_recv()
                far.start()

            @pl.when(core == 0)
            def _():
                from_relay[0].wait_recv()
                from_relay[1].wait_recv()
            near.wait_recv()
            far.wait_recv()

        column = lax.broadcasted_iota(jnp.int32, (1, SEG), 1) // BLK
        open_column = jnp.zeros((1, SEG), jnp.int32)
        for e in range(RET):
            block = retrieval[0, e]
            xmem[e * BLK : (e + 1) * BLK] = buf[RET + block]
            usable = jnp.where(block // 8 + 1 <= me, 1, 0)
            open_column = jnp.where(column == e, usable, open_column)
        project(mkey, xmem, vk, D)
        project(mvalue, xmem, vv, D)

        def memory_part(chunk, carry):
            rows = rows_of(chunk)
            partial_attention(
                qtok.at[rows], mkey, mvalue, acc.at[rows], peak.at[rows],
                jnp.broadcast_to(open_column > 0, (ROWS, SEG)), False, att.at[rows],
            )
            return carry

        lax.fori_loop(0, CHUNKS, memory_part, 0)
        loads["wo"].wait()

        def out_part(n, carry):
            cols = pl.ds(pl.multiple_of(n * 512, 512), 512)
            xmem[:, cols] = (own[:, cols].astype(F32) + dot(att[...], vo[:, cols])).astype(BF16)
            return carry

        lax.fori_loop(0, 2, out_part, 0)
        store_mixed = pltpu.make_async_copy(xmem, mixed, out_sem.at[1])
        store_mixed.start()
        if comm:
            hop.wait_send()
            near.wait_send()
            far.wait_send()
            for k in range(2):
                to_relay[k].wait_send()
                from_relay[k].wait_send()
            for sweep in range(ITERS):
                for chunk in range(CHUNKS):
                    state_copy(sweep, chunk).wait_send()
        store_state.wait()
        store_mixed.wait()

    return kernel


def make_call(count, comm):
    square = pltpu.VMEM((D, D), BF16)
    wide = pltpu.VMEM((D, 2 * D), BF16)
    seg = pltpu.VMEM((SEG, D), BF16)
    return pl.pallas_call(
        make_kernel(count, comm),
        name="layer",
        out_shape=(jax.ShapeDtypeStruct((SEG, D), BF16), jax.ShapeDtypeStruct((SEG, D), BF16)),
        in_specs=[pl.BlockSpec(memory_space=pl.ANY)] * 10
        + [pl.BlockSpec(memory_space=pltpu.VMEM)]
        + [pl.BlockSpec(memory_space=pltpu.SMEM)] * 2,
        out_specs=(pl.BlockSpec(memory_space=pl.ANY),) * 2,
        scratch_shapes=[
            pltpu.VMEM((5 * RET, BLK, D), BF16), seg, pltpu.VMEM((RET, BLK, D), BF16),
            square, square, square, square, square, wide, wide,
            seg, seg, seg, seg, pltpu.VMEM((SEG, 2 * D), BF16), seg, seg,
            seg, seg, pltpu.VMEM((ITERS, SEG, D), BF16), pltpu.VMEM((ITERS, SEG, D), BF16), seg, seg, seg,
            pltpu.VMEM((SEG, 2 * D), F32), pltpu.VMEM((SEG, D), F32),
            pltpu.SemaphoreType.DMA((10,)), pltpu.SemaphoreType.DMA((2,)),
            pltpu.SemaphoreType.DMA((7 + ITERS * CHUNKS,)), pltpu.SemaphoreType.DMA((7 + ITERS * CHUNKS,)),
        ],
        compiler_params=pltpu.CompilerParams(
            collective_id=0 if comm else None, has_side_effects=True, vmem_limit_bytes=62 << 20
        ),
    )


def solution(mesh):
    count = mesh.shape["seq"]

    def per_device(tokens, init_state, w_query, w_key, w_value, w_out, w_query_state, w_cand_gate,
                   w_state_kv, gate_bias, mixing, retrieval):
        return make_call(count, True)(
            tokens.reshape(RET, BLK, D), tokens, init_state, w_query, w_key, w_value, w_out, w_query_state, w_cand_gate,
            w_state_kv, gate_bias.reshape(1, -1), mixing, retrieval,
        )

    return jax.shard_map(
        per_device,
        mesh=mesh,
        in_specs=(P("seq", None), P(), P(), P(), P(), P(), P(), P(), P(), P(), P(), P("seq", None)),
        out_specs=(P("seq", None), P("seq", None)),
        check_vma=False,
    )
```

profile of v0, /device:TPU:0, one launch (start us, length us, event | category | flops | bytes accessed | tf_op | source)
XLA Modules:
  0.0 94.1 jit_solution(9885903623224325879)
XLA Ops:
  0.6 90.1 %layer.1 = (bf16[512,1024]{1,0:T(8,128)(2,1)}, bf16[512,1024]{1,0:T(8,128)(2,1)}) custom-call(bf16[8,64,1024]{2,1,0:T(8,128)(2,1)} %bitcast.2, bf16[512,1024]{1,0:T(8,128)(2,1)} %tokens_flat.1, bf16[512,1024]{1,0:T(8,128)(2,1)} %init.1, bf16[1024,1024]{1,0:T(8,128)(2,1)} %wq.1, bf16[1024,1024]{1,0:T(8,128)(2,1)} %wk.1, bf16[1024,1024]{1,0:T(8,128)(2,1)} %wv.1, ...), custom_call_target="tpu_custom_call" | custom-call | tf_op jit(solution)/shard_map/layer/pallas_call | solution.py:369
  90.8 0.0 copy-start
  90.8 2.4 %copy.16 = bf16[512,1024]{1,0:T(8,128)(2,1)} copy(bf16[512,1024]{1,0:T(8,128)(2,1)} %get-tuple-element.4) | data formatting | bytes 2097152
  93.1 0.0 copy-done
  93.1 1.0 %copy.17 = bf16[512,1024]{1,0:T(8,128)(2,1)} copy(bf16[512,1024]{1,0:T(8,128)(2,1)S(1)} %copy-done) | data formatting | bytes 2097152
Async XLA Ops:
  90.8 2.4 %copy-start = (bf16[512,1024]{1,0:T(8,128)(2,1)S(1)}, bf16[512,1024]{1,0:T(8,128)(2,1)}, u32[]{:S(2)}) copy-start(bf16[512,1024]{1,0:T(8,128)(2,1)} %get-tuple-element.5) | copy-start | bytes 3145732
where the time goes:
time: 94.3 us; the launch traced here: 94.1 us
  Pallas kernels  90.1 us (96%)
  local copies, waits for them, and re-layouts  3.32 us (4%)
    pallas_call x1, Pallas kernels, per_device(): make_call(count, True)  90.1 us
    unnamed x4, local copies, waits for them, and re-layouts  3.32 us

commit v1 on v0

--- a/solution.py
+++ b/solution.py
@@ -14,7 +14,6 @@
 ITERS = 2
 ROWS = 256
 CHUNKS = SEG // ROWS
-HALF = RET // 2
 LOG2E = 1.4426950408889634
 SCALE = LOG2E / HW**0.5
 NEG = -1e30
@@ -58,9 +57,9 @@
         out[:, cols] = (ol[:, :HW] / ol[:, HW:]).astype(BF16)
 
 
-def partial_attention(query, keys, values, acc, peak, mask, first, out):
+def partial_attention(query, keys, values, acc, peak, mask, first, out, heads=range(HEADS)):
     count = query.shape[0]
-    for h in range(HEADS):
+    for h in heads:
         cols = slice(h * HW, (h + 1) * HW)
         wide = slice(h * 2 * HW, (h + 1) * 2 * HW)
         s = dot_nt(query[:, cols], keys[:, cols]) * SCALE
@@ -118,9 +117,8 @@
         sibling = me + 1 - 2 * core
         nxt, prev = wrap(me + 1), wrap(me - 1)
         two_on, two_back = wrap(me + 2), wrap(me - 2)
-        relay_to, relay_from = minus_y(me), plus_y(me)
-        final_to = wrap(relay_from + 4)
-        final_from = minus_y(wrap(me - 4))
+        relay_to = wrap(minus_y(me) + me // 2 % 4 // 2 * (1 - me // 2 % 2) * 8)
+        relay_from = wrap(plus_y(me) - (me // 2 + 1) % 4 // 2 * (1 - (me // 2 + 1) % 2) * 8)
 
         loads = {}
 
@@ -145,37 +143,62 @@
                 device_id=(device,), device_id_type=MESH,
             )
 
-        def slot(d, half=None):
-            if half is None:
-                return buf.at[pl.ds(d * RET, RET)]
-            return buf.at[pl.ds(d * RET + half * HALF, HALF)]
-
-        hop = remote(0, slot(0), slot(2), two_on)
-        to_relay = [remote(1 + k, slot(0, k), relay.at[pl.ds(k * HALF, HALF)], relay_to) for k in range(2)]
-        from_relay = [remote(3 + k, relay.at[pl.ds(k * HALF, HALF)], slot(4, k), final_to) for k in range(2)]
-        near = remote(5, buf.at[pl.ds(core * 2 * RET, RET)], slot(1), sibling)
-        far = remote(6, buf.at[pl.ds((core + 1) * 2 * RET, RET)], slot(3), sibling)
+        def slot(d):
+            return buf.at[pl.ds(d * RET, RET)]
+
+        def part_of(d, k, parts):
+            return buf.at[pl.ds(d * RET + k * (RET // parts), RET // parts)]
+
+        hop = [remote(k, part_of(0, k, 4), part_of(2, k, 4), two_on) for k in range(4)]
+        half = RET // 2
+        to_relay = [remote(4 + k, part_of(0, k, 2), relay.at[pl.ds(k * half, half)], relay_to) for k in range(2)]
+        from_relay = [remote(6 + k, relay.at[pl.ds(k * half, half)], part_of(4, k, 2), relay_to) for k in range(2)]
+        near = [remote(8 + k, part_of(2 * core, k, 2), part_of(1, k, 2), sibling) for k in range(2)]
+        far = [remote(10 + k, part_of(2 + 2 * core, k, 2), part_of(3, k, 2), sibling) for k in range(2)]
+        fill_two = pltpu.make_async_copy(tokens, slot(2), load_sem.at[10])
+        fill_four = pltpu.make_async_copy(tokens, slot(4), load_sem.at[11])
+        hop_out, hop_in = me < count - 2, me >= 2
+        relay_out, relay_pass, relay_in = me < count - 4, relay_from < count - 4, me >= 4
+
+        def start_hop(who, parts):
+            @pl.when(jnp.logical_and(core == who, hop_out))
+            def _():
+                for k in parts:
+                    hop[k].start()
 
         def state_copy(sweep, chunk):
             return remote(
-                7 + sweep * CHUNKS + chunk, outs.at[sweep, rows_of(chunk)],
+                12 + sweep * CHUNKS + chunk, outs.at[sweep, rows_of(chunk)],
                 shifted.at[sweep, rows_of(chunk)], nxt,
             )
 
         if comm:
             barrier = pltpu.get_barrier_semaphore()
-            for source in (sibling, prev, two_back, relay_from, final_from):
+            for source in (sibling, prev, two_back, relay_from):
                 pl.semaphore_signal(barrier, inc=1, device_id=(source,), device_id_type=MESH)
-            pl.semaphore_wait(barrier, 5)
+            pl.semaphore_wait(barrier, 4)
         loads["tokens"].wait()
         if comm:
-            to_relay[0].start()
-            to_relay[1].start()
+            start_hop(0, (0, 1))
+            start_hop(1, (0,))
+
+            @pl.when(relay_out)
+            def _():
+                for part in to_relay:
+                    part.start()
 
             @pl.when(core == 0)
             def _():
-                hop.start()
-                near.start()
+                for part in near:
+                    part.start()
+
+            @pl.when(me < 2)
+            def _():
+                fill_two.start()
+
+            @pl.when(me < 4)
+            def _():
+                fill_four.start()
 
         loads["own"].wait()
         loads["wk"].wait()
@@ -194,7 +217,13 @@
                 rows = rows_of(chunk)
                 if sweep > 0:
                     if comm:
-                        state_copy(sweep - 1, chunk).wait_recv()
+                        @pl.when(me > 0)
+                        def _():
+                            state_copy(sweep - 1, chunk).wait_recv()
+
+                        @pl.when(chunk == 0)
+                        def _():
+                            start_hop(0, (1 + sweep,))
                     base = state0[rows].astype(F32)
                     moved = jnp.where(first_segment, base, shifted[sweep - 1, rows].astype(F32))
                     if sweep == 1:
@@ -207,7 +236,7 @@
                     ).astype(BF16)
                 project(query.at[rows], source.at[rows], vqs, D)
                 if sweep < ITERS and comm:
-                    @pl.when(chunk > 0)
+                    @pl.when(jnp.logical_and(chunk > 0, me < count - 1))
                     def _():
                         state_copy(sweep, chunk - 1).start()
                 self_attention(query.at[rows], key, value, att.at[rows])
@@ -216,47 +245,47 @@
                     def _():
                         loads["wcg"].wait()
                 gate(att.at[rows], vcg, bias, source.at[rows], (outs.at[sweep] if sweep < ITERS else final).at[rows])
+                if sweep == 1 and comm:
+                    @pl.when(jnp.logical_and(chunk == 0, relay_pass))
+                    def _():
+                        for k in range(2):
+                            to_relay[k].wait_recv()
+                            from_relay[k].start()
                 return carry
 
             lax.fori_loop(0, CHUNKS, chunk_body, 0)
 
         def last_send(sweep):
             if comm:
-                state_copy(sweep, CHUNKS - 1).start()
-
-        def local_attention(chunk):
+                @pl.when(me < count - 1)
+                def _():
+                    state_copy(sweep, CHUNKS - 1).start()
+
+        def local_attention(chunk, heads):
             rows = slice(chunk * ROWS, (chunk + 1) * ROWS)
             width = (chunk + 1) * ROWS
             row = lax.broadcasted_iota(jnp.int32, (ROWS, width), 0) + chunk * ROWS
             col = lax.broadcasted_iota(jnp.int32, (ROWS, width), 1)
             partial_attention(
                 qtok.at[rows], key.at[slice(0, width)], value.at[slice(0, width)],
-                acc.at[rows], peak.at[rows], col <= row, True, None,
+                acc.at[rows], peak.at[rows], col <= row, True, None, heads,
             )
 
         forward_state(0)
         loads["wq"].wait()
-        project(qtok, own, vq, D)
-        last_send(0)
-        if comm:
-            to_relay[0].wait_recv()
-            from_relay[0].start()
-        local_attention(0)
+        half_columns = D // 2
+        for n in range(2):
+            cols = slice(n * half_columns, (n + 1) * half_columns)
+            qtok[:, cols] = dot(own[...], vq[:, cols]).astype(BF16)
+            if n == 0:
+                last_send(0)
+        local_attention(0, range(HEADS))
         forward_state(1)
-        if comm:
-            to_relay[1].wait_recv()
-            from_relay[1].start()
-        local_attention(1)
+        local_attention(1, range(2))
         last_send(1)
         if comm:
-            @pl.when(core == 1)
-            def _():
-                hop.start()
-
-            @pl.when(core == 0)
-            def _():
-                hop.wait_recv()
-                far.start()
+            start_hop(1, (1, 2, 3))
+        local_attention(1, range(2, HEADS))
         forward_state(2)
         store_state = pltpu.make_async_copy(final, new_state, out_sem.at[0])
         loads["wskv"].wait()
@@ -274,20 +303,40 @@
         lax.fori_loop(0, CHUNKS, state_part, 0)
 
         if comm:
-            @pl.when(core == 1)
-            def _():
-                hop.wait_recv()
-                near.start()
-                from_relay[0].wait_recv()
-                from_relay[1].wait_recv()
-                far.start()
-
-            @pl.when(core == 0)
-            def _():
-                from_relay[0].wait_recv()
-                from_relay[1].wait_recv()
-            near.wait_recv()
-            far.wait_recv()
+            for k in range(2):
+                @pl.when(hop_in)
+                def _():
+                    hop[2 * k].wait_recv()
+                    hop[2 * k + 1].wait_recv()
+
+                if k == 0:
+                    @pl.when(me < 2)
+                    def _():
+                        fill_two.wait()
+
+                    @pl.when(me < 4)
+                    def _():
+                        fill_four.wait()
+
+                @pl.when(core == 0)
+                def _():
+                    far[k].start()
+
+                @pl.when(core == 1)
+                def _():
+                    near[k].start()
+
+                @pl.when(relay_in)
+                def _():
+                    from_relay[k].wait_recv()
+
+                @pl.when(core == 1)
+                def _():
+                    far[k].start()
+
+            for k in range(2):
+                near[k].wait_recv()
+                far[k].wait_recv()
 
         column = lax.broadcasted_iota(jnp.int32, (1, SEG), 1) // BLK
         open_column = jnp.zeros((1, SEG), jnp.int32)
@@ -319,15 +368,31 @@
         store_mixed = pltpu.make_async_copy(xmem, mixed, out_sem.at[1])
         store_mixed.start()
         if comm:
-            hop.wait_send()
-            near.wait_send()
-            far.wait_send()
             for k in range(2):
-                to_relay[k].wait_send()
-                from_relay[k].wait_send()
-            for sweep in range(ITERS):
-                for chunk in range(CHUNKS):
-                    state_copy(sweep, chunk).wait_send()
+                near[k].wait_send()
+                far[k].wait_send()
+
+            @pl.when(hop_out)
+            def _():
+                for part in hop:
+                    part.wait_send()
+
+            @pl.when(relay_out)
+            def _():
+                for part in to_relay:
+                    part.wait_send()
+
+            @pl.when(relay_pass)
+            def _():
+                for part in from_relay:
+                    part.wait_send()
+
+            @pl.when(me < count - 1)
+            def _():
+                for sweep in range(ITERS):
+                    for chunk in range(CHUNKS):
+                        state_copy(sweep, chunk).wait_send()
+
         store_state.wait()
         store_mixed.wait()
 
@@ -352,8 +417,8 @@
             seg, seg, seg, seg, pltpu.VMEM((SEG, 2 * D), BF16), seg, seg,
             seg, seg, pltpu.VMEM((ITERS, SEG, D), BF16), pltpu.VMEM((ITERS, SEG, D), BF16), seg, seg, seg,
             pltpu.VMEM((SEG, 2 * D), F32), pltpu.VMEM((SEG, D), F32),
-            pltpu.SemaphoreType.DMA((10,)), pltpu.SemaphoreType.DMA((2,)),
-            pltpu.SemaphoreType.DMA((7 + ITERS * CHUNKS,)), pltpu.SemaphoreType.DMA((7 + ITERS * CHUNKS,)),
+            pltpu.SemaphoreType.DMA((12,)), pltpu.SemaphoreType.DMA((2,)),
+            pltpu.SemaphoreType.DMA((12 + ITERS * CHUNKS,)), pltpu.SemaphoreType.DMA((12 + ITERS * CHUNKS,)),
         ],
         compiler_params=pltpu.CompilerParams(
             collective_id=0 if comm else None, has_side_effects=True, vmem_limit_bytes=62 << 20

time: 94.3 us -> 74.5 us (0.79)
  the two profiles are of different devices: /device:TPU:0 before, /device:TPU:97 now
where the time goes in v1:
time: 74.5 us; the launch traced here: 74.4 us
  Pallas kernels  70.4 us (94%)
  local copies, waits for them, and re-layouts  3.32 us (4%)
    pallas_call x1, Pallas kernels, per_device(): make_call(count, True)  70.4 us
    unnamed x4, local copies, waits for them, and re-layouts  3.32 us

profile of v1, /device:TPU:97, one launch (start us, length us, event | category | flops | bytes accessed | tf_op | source)
XLA Modules:
  0.0 74.4 jit_solution(18299617214270248116)
XLA Ops:
  0.6 70.4 %layer.1 = (bf16[512,1024]{1,0:T(8,128)(2,1)}, bf16[512,1024]{1,0:T(8,128)(2,1)}) custom-call(bf16[8,64,1024]{2,1,0:T(8,128)(2,1)} %bitcast.2, bf16[512,1024]{1,0:T(8,128)(2,1)} %tokens_flat.1, bf16[512,1024]{1,0:T(8,128)(2,1)} %init.1, bf16[1024,1024]{1,0:T(8,128)(2,1)} %wq.1, bf16[1024,1024]{1,0:T(8,128)(2,1)} %wk.1, bf16[1024,1024]{1,0:T(8,128)(2,1)} %wv.1, ...), custom_call_target="tpu_custom_call" | custom-call | tf_op jit(solution)/shard_map/layer/pallas_call | solution.py:434
  71.0 0.0 copy-start
  71.0 2.4 %copy.16 = bf16[512,1024]{1,0:T(8,128)(2,1)} copy(bf16[512,1024]{1,0:T(8,128)(2,1)} %get-tuple-element.4) | data formatting | bytes 2097152
  73.4 0.0 copy-done
  73.4 1.0 %copy.17 = bf16[512,1024]{1,0:T(8,128)(2,1)} copy(bf16[512,1024]{1,0:T(8,128)(2,1)S(1)} %copy-done) | data formatting | bytes 2097152
Async XLA Ops:
  71.0 2.4 %copy-start = (bf16[512,1024]{1,0:T(8,128)(2,1)S(1)}, bf16[512,1024]{1,0:T(8,128)(2,1)}, u32[]{:S(2)}) copy-start(bf16[512,1024]{1,0:T(8,128)(2,1)} %get-tuple-element.5) | copy-start | bytes 3145732

commit v2 on v1

--- a/solution.py
+++ b/solution.py
@@ -99,7 +99,7 @@
         mixed, new_state,
         buf, own, relay, vq, vk, vv, vo, vqs, vcg, vskv,
         key, value, mkey, mvalue, skv, qtok, xmem,
-        state0, guess, outs, shifted, query, att, final, acc, peak,
+        state0, guess, outs, shifted, lent, query, att, final, acc, peak,
         load_sem, out_sem, send_sem, recv_sem,
     ):
         me = lax.axis_index("seq") if comm else jnp.int32(7)
@@ -166,11 +166,47 @@
                 for k in parts:
                     hop[k].start()
 
-        def state_copy(sweep, chunk):
-            return remote(
-                12 + sweep * CHUNKS + chunk, outs.at[sweep, rows_of(chunk)],
-                shifted.at[sweep, rows_of(chunk)], nxt,
+        def half_of(chunk, k):
+            return pl.ds(pl.multiple_of(chunk * ROWS + k * (ROWS // 2), ROWS // 2), ROWS // 2)
+
+        first_sem, second_sem, third_sem = 12, 12 + ITERS * CHUNKS, 12 + 2 * ITERS * CHUNKS
+
+        def direct(sweep, chunk):
+            rows = half_of(chunk, 0)
+            return remote(first_sem + sweep * CHUNKS + chunk, outs.at[sweep, rows], shifted.at[sweep, rows], nxt)
+
+        def beside(sweep, chunk):
+            rows = half_of(chunk, 1)
+            return remote(second_sem + sweep * CHUNKS + chunk, outs.at[sweep, rows], shifted.at[sweep, rows], nxt)
+
+        def lend(sweep, chunk):
+            n = third_sem + sweep * CHUNKS + chunk
+            return remote(n, outs.at[sweep, half_of(chunk, 1)], lent.at[sweep * CHUNKS + chunk], sibling)
+
+        def pass_on(sweep, chunk):
+            n = sweep * CHUNKS + chunk
+            return pltpu.make_async_remote_copy(
+                src_ref=lent.at[n], dst_ref=shifted.at[sweep, half_of(chunk, 1)],
+                send_sem=send_sem.at[third_sem + n], recv_sem=recv_sem.at[second_sem + n],
+                device_id=(two_on,), device_id_type=MESH,
             )
+
+        def send_state(sweep, chunk):
+            @pl.when(core == 0)
+            def _():
+                direct(sweep, chunk).start()
+                beside(sweep, chunk).start()
+
+            @pl.when(jnp.logical_and(core == 1, me < count - 1))
+            def _():
+                lend(sweep, chunk).start()
+                direct(sweep, chunk).start()
+
+        def pass_state(sweep, chunk):
+            @pl.when(jnp.logical_and(core == 0, me < count - 2))
+            def _():
+                lend(sweep, chunk).wait_recv()
+                pass_on(sweep, chunk).start()
 
         if comm:
             barrier = pltpu.get_barrier_semaphore()
@@ -219,11 +255,13 @@
                     if comm:
                         @pl.when(me > 0)
                         def _():
-                            state_copy(sweep - 1, chunk).wait_recv()
-
-                        @pl.when(chunk == 0)
-                        def _():
-                            start_hop(0, (1 + sweep,))
+                            direct(sweep - 1, chunk).wait_recv()
+                            beside(sweep - 1, chunk).wait_recv()
+
+                        if sweep == 1:
+                            @pl.when(chunk == 0)
+                            def _():
+                                start_hop(1, (1,))
                     base = state0[rows].astype(F32)
                     moved = jnp.where(first_segment, base, shifted[sweep - 1, rows].astype(F32))
                     if sweep == 1:
@@ -236,10 +274,14 @@
                     ).astype(BF16)
                 project(query.at[rows], source.at[rows], vqs, D)
                 if sweep < ITERS and comm:
-                    @pl.when(jnp.logical_and(chunk > 0, me < count - 1))
-                    def _():
-                        state_copy(sweep, chunk - 1).start()
+                    @pl.when(chunk > 0)
+                    def _():
+                        send_state(sweep, chunk - 1)
                 self_attention(query.at[rows], key, value, att.at[rows])
+                if sweep < ITERS and comm:
+                    @pl.when(chunk > 0)
+                    def _():
+                        pass_state(sweep, chunk - 1)
                 if sweep == 0:
                     @pl.when(chunk == 0)
                     def _():
@@ -254,12 +296,6 @@
                 return carry
 
             lax.fori_loop(0, CHUNKS, chunk_body, 0)
-
-        def last_send(sweep):
-            if comm:
-                @pl.when(me < count - 1)
-                def _():
-                    state_copy(sweep, CHUNKS - 1).start()
 
         def local_attention(chunk, heads):
             rows = slice(chunk * ROWS, (chunk + 1) * ROWS)
@@ -278,13 +314,19 @@
             cols = slice(n * half_columns, (n + 1) * half_columns)
             qtok[:, cols] = dot(own[...], vq[:, cols]).astype(BF16)
             if n == 0:
-                last_send(0)
-        local_attention(0, range(HEADS))
+                if comm:
+                    send_state(0, CHUNKS - 1)
+        local_attention(0, range(4))
+        if comm:
+            pass_state(0, CHUNKS - 1)
+        local_attention(0, range(4, HEADS))
         forward_state(1)
         local_attention(1, range(2))
-        last_send(1)
         if comm:
-            start_hop(1, (1, 2, 3))
+            send_state(1, CHUNKS - 1)
+            start_hop(1, (2, 3))
+            pass_state(1, CHUNKS - 1)
+            start_hop(0, (2, 3))
         local_attention(1, range(2, HEADS))
         forward_state(2)
         store_state = pltpu.make_async_copy(final, new_state, out_sem.at[0])
@@ -387,11 +429,23 @@
                 for part in from_relay:
                     part.wait_send()
 
-            @pl.when(me < count - 1)
-            def _():
-                for sweep in range(ITERS):
-                    for chunk in range(CHUNKS):
-                        state_copy(sweep, chunk).wait_send()
+            for sweep in range(ITERS):
+                for chunk in range(CHUNKS):
+                    @pl.when(me < count - 1)
+                    def _():
+                        direct(sweep, chunk).wait_send()
+
+                    @pl.when(core == 0)
+                    def _():
+                        beside(sweep, chunk).wait_send()
+
+                    @pl.when(jnp.logical_and(core == 1, me < count - 1))
+                    def _():
+                        lend(sweep, chunk).wait_send()
+
+                    @pl.when(jnp.logical_and(core == 0, me < count - 2))
+                    def _():
+                        pass_on(sweep, chunk).wait_send()
 
         store_state.wait()
         store_mixed.wait()
@@ -415,10 +469,11 @@
             pltpu.VMEM((5 * RET, BLK, D), BF16), seg, pltpu.VMEM((RET, BLK, D), BF16),
             square, square, square, square, square, wide, wide,
             seg, seg, seg, seg, pltpu.VMEM((SEG, 2 * D), BF16), seg, seg,
-            seg, seg, pltpu.VMEM((ITERS, SEG, D), BF16), pltpu.VMEM((ITERS, SEG, D), BF16), seg, seg, seg,
+            seg, seg, pltpu.VMEM((ITERS, SEG, D), BF16), pltpu.VMEM((ITERS, SEG, D), BF16),
+            pltpu.VMEM((ITERS * CHUNKS, ROWS // 2, D), BF16), seg, seg, seg,
             pltpu.VMEM((SEG, 2 * D), F32), pltpu.VMEM((SEG, D), F32),
             pltpu.SemaphoreType.DMA((12,)), pltpu.SemaphoreType.DMA((2,)),
-            pltpu.SemaphoreType.DMA((12 + ITERS * CHUNKS,)), pltpu.SemaphoreType.DMA((12 + ITERS * CHUNKS,)),
+            pltpu.SemaphoreType.DMA((12 + 3 * ITERS * CHUNKS,)), pltpu.SemaphoreType.DMA((12 + 3 * ITERS * CHUNKS,)),
         ],
         compiler_params=pltpu.CompilerParams(
             collective_id=0 if comm else None, has_side_effects=True, vmem_limit_bytes=62 << 20

time: 74.5 us -> 76.1 us (1.021)
  Pallas kernels: 70.4 us -> 72 us
    pallas_call x1, Pallas kernels: 70.4 us -> 72 us  [per_device(): make_call(count, True)]
where the time goes in v2:
time: 76.1 us; the launch traced here: 76 us
  Pallas kernels  72 us (95%)
  local copies, waits for them, and re-layouts  3.32 us (4%)
    pallas_call x1, Pallas kernels, per_device(): make_call(count, True)  72 us
    unnamed x4, local copies, waits for them, and re-layouts  3.32 us

profile of v2, /device:TPU:97, one launch (start us, length us, event | category | flops | bytes accessed | tf_op | source)
XLA Modules:
  0.0 76.0 jit_solution(4544195341191677777)
XLA Ops:
  0.6 72.0 %layer.1 = (bf16[512,1024]{1,0:T(8,128)(2,1)}, bf16[512,1024]{1,0:T(8,128)(2,1)}) custom-call(bf16[8,64,1024]{2,1,0:T(8,128)(2,1)} %bitcast.2, bf16[512,1024]{1,0:T(8,128)(2,1)} %tokens_flat.1, bf16[512,1024]{1,0:T(8,128)(2,1)} %init.1, bf16[1024,1024]{1,0:T(8,128)(2,1)} %wq.1, bf16[1024,1024]{1,0:T(8,128)(2,1)} %wk.1, bf16[1024,1024]{1,0:T(8,128)(2,1)} %wv.1, ...), custom_call_target="tpu_custom_call" | custom-call | tf_op jit(solution)/shard_map/layer/pallas_call | solution.py:489
  72.6 0.0 copy-start
  72.6 2.4 %copy.16 = bf16[512,1024]{1,0:T(8,128)(2,1)} copy(bf16[512,1024]{1,0:T(8,128)(2,1)} %get-tuple-element.4) | data formatting | bytes 2097152
  75.0 0.0 copy-done
  75.0 1.0 %copy.17 = bf16[512,1024]{1,0:T(8,128)(2,1)} copy(bf16[512,1024]{1,0:T(8,128)(2,1)S(1)} %copy-done) | data formatting | bytes 2097152
Async XLA Ops:
  72.6 2.4 %copy-start = (bf16[512,1024]{1,0:T(8,128)(2,1)S(1)}, bf16[512,1024]{1,0:T(8,128)(2,1)}, u32[]{:S(2)}) copy-start(bf16[512,1024]{1,0:T(8,128)(2,1)} %get-tuple-element.5) | copy-start | bytes 3145732

commit v3 on v1

--- a/solution.py
+++ b/solution.py
@@ -95,9 +95,9 @@
 
 def make_kernel(count, comm):
     def kernel(
-        tokens, tokens_flat, init, wq, wk, wv, wo, wqs, wcg, wskv, bias, mixing, retrieval,
-        mixed, new_state,
-        buf, own, relay, vq, vk, vv, vo, vqs, vcg, vskv,
+        tokens, tokens_flat, init, wq, wk, wv, wqs, wcg, wskv, bias, mixing, retrieval,
+        attended, new_state,
+        buf, own, relay, vq, vk, vv, vqs, vcg, vskv,
         key, value, mkey, mvalue, skv, qtok, xmem,
         state0, guess, outs, shifted, query, att, final, acc, peak,
         load_sem, out_sem, send_sem, recv_sem,
@@ -129,13 +129,6 @@
         load("tokens", 0, tokens, buf.at[pl.ds(0, RET)])
         load("own", 9, tokens_flat, own)
         load("wk", 1, wk, vk)
-        load("wv", 2, wv, vv)
-        load("init", 3, init, state0)
-        load("wqs", 4, wqs, vqs)
-        load("wcg", 5, wcg, vcg)
-        load("wq", 6, wq, vq)
-        load("wskv", 7, wskv, vskv)
-        load("wo", 8, wo, vo)
 
         def remote(n, src, dst, device):
             return pltpu.make_async_remote_copy(
@@ -153,8 +146,8 @@
         half = RET // 2
         to_relay = [remote(4 + k, part_of(0, k, 2), relay.at[pl.ds(k * half, half)], relay_to) for k in range(2)]
         from_relay = [remote(6 + k, relay.at[pl.ds(k * half, half)], part_of(4, k, 2), relay_to) for k in range(2)]
-        near = [remote(8 + k, part_of(2 * core, k, 2), part_of(1, k, 2), sibling) for k in range(2)]
-        far = [remote(10 + k, part_of(2 + 2 * core, k, 2), part_of(3, k, 2), sibling) for k in range(2)]
+        near = [remote(8 + k, part_of(2 * core, k, 4), part_of(1, k, 4), sibling) for k in range(4)]
+        far = [remote(12 + k, part_of(2 + 2 * core, k, 2), part_of(3, k, 2), sibling) for k in range(2)]
         fill_two = pltpu.make_async_copy(tokens, slot(2), load_sem.at[10])
         fill_four = pltpu.make_async_copy(tokens, slot(4), load_sem.at[11])
         hop_out, hop_in = me < count - 2, me >= 2
@@ -166,9 +159,41 @@
                 for k in parts:
                     hop[k].start()
 
+        def take_hop(parts):
+            @pl.when(hop_in)
+            def _():
+                for k in parts:
+                    hop[k].wait_recv()
+
+        def exchange(quarters, halves):
+            @pl.when(core == 1)
+            def _():
+                take_hop(quarters)
+                for k in quarters:
+                    near[k].start()
+
+            @pl.when(core == 0)
+            def _():
+                for k in halves:
+                    take_hop((2 * k, 2 * k + 1))
+                    far[k].start()
+
+            for k in halves:
+                if k > 0:
+                    relay_arrived(k)
+
+        def relay_arrived(k):
+            @pl.when(relay_in)
+            def _():
+                from_relay[k].wait_recv()
+
+            @pl.when(core == 1)
+            def _():
+                far[k].start()
+
         def state_copy(sweep, chunk):
             return remote(
-                12 + sweep * CHUNKS + chunk, outs.at[sweep, rows_of(chunk)],
+                14 + sweep * CHUNKS + chunk, outs.at[sweep, rows_of(chunk)],
                 shifted.at[sweep, rows_of(chunk)], nxt,
             )
 
@@ -200,11 +225,16 @@
             def _():
                 fill_four.start()
 
+        load("wv", 2, wv, vv)
+        load("init", 3, init, state0)
+        load("wqs", 4, wqs, vqs)
+        load("wcg", 5, wcg, vcg)
         loads["own"].wait()
         loads["wk"].wait()
         project(key, own, vk, D)
         loads["wv"].wait()
         project(value, own, vv, D)
+        load("wq", 6, wq, vq)
         loads["init"].wait()
         loads["wqs"].wait()
 
@@ -240,17 +270,17 @@
                     def _():
                         state_copy(sweep, chunk - 1).start()
                 self_attention(query.at[rows], key, value, att.at[rows])
+                if sweep == 1 and comm:
+                    @pl.when(jnp.logical_and(chunk == 1, relay_pass))
+                    def _():
+                        for k in range(2):
+                            to_relay[k].wait_recv()
+                            from_relay[k].start()
                 if sweep == 0:
                     @pl.when(chunk == 0)
                     def _():
                         loads["wcg"].wait()
                 gate(att.at[rows], vcg, bias, source.at[rows], (outs.at[sweep] if sweep < ITERS else final).at[rows])
-                if sweep == 1 and comm:
-                    @pl.when(jnp.logical_and(chunk == 0, relay_pass))
-                    def _():
-                        for k in range(2):
-                            to_relay[k].wait_recv()
-                            from_relay[k].start()
                 return carry
 
             lax.fori_loop(0, CHUNKS, chunk_body, 0)
@@ -272,6 +302,7 @@
             )
 
         forward_state(0)
+        load("wskv", 7, wskv, vskv)
         loads["wq"].wait()
         half_columns = D // 2
         for n in range(2):
@@ -286,11 +317,23 @@
         if comm:
             start_hop(1, (1, 2, 3))
         local_attention(1, range(2, HEADS))
+        if comm:
+            @pl.when(me < 2)
+            def _():
+                fill_two.wait()
+
+            @pl.when(me < 4)
+            def _():
+                fill_four.wait()
+
+            exchange(range(1), (0,))
         forward_state(2)
         store_state = pltpu.make_async_copy(final, new_state, out_sem.at[0])
         loads["wskv"].wait()
         project(skv, guess, vskv, 2 * D)
         store_state.start()
+        if comm:
+            relay_arrived(0)
 
         def state_part(chunk, carry):
             rows = rows_of(chunk)
@@ -303,40 +346,9 @@
         lax.fori_loop(0, CHUNKS, state_part, 0)
 
         if comm:
-            for k in range(2):
-                @pl.when(hop_in)
-                def _():
-                    hop[2 * k].wait_recv()
-                    hop[2 * k + 1].wait_recv()
-
-                if k == 0:
-                    @pl.when(me < 2)
-                    def _():
-                        fill_two.wait()
-
-                    @pl.when(me < 4)
-                    def _():
-                        fill_four.wait()
-
-                @pl.when(core == 0)
-                def _():
-                    far[k].start()
-
-                @pl.when(core == 1)
-                def _():
-                    near[k].start()
-
-                @pl.when(relay_in)
-                def _():
-                    from_relay[k].wait_recv()
-
-                @pl.when(core == 1)
-                def _():
-                    far[k].start()
-
-            for k in range(2):
-                near[k].wait_recv()
-                far[k].wait_recv()
+            exchange(range(1, 4), (1,))
+            for part in near + far:
+                part.wait_recv()
 
         column = lax.broadcasted_iota(jnp.int32, (1, SEG), 1) // BLK
         open_column = jnp.zeros((1, SEG), jnp.int32)
@@ -357,20 +369,11 @@
             return carry
 
         lax.fori_loop(0, CHUNKS, memory_part, 0)
-        loads["wo"].wait()
-
-        def out_part(n, carry):
-            cols = pl.ds(pl.multiple_of(n * 512, 512), 512)
-            xmem[:, cols] = (own[:, cols].astype(F32) + dot(att[...], vo[:, cols])).astype(BF16)
-            return carry
-
-        lax.fori_loop(0, 2, out_part, 0)
-        store_mixed = pltpu.make_async_copy(xmem, mixed, out_sem.at[1])
-        store_mixed.start()
-        if comm:
-            for k in range(2):
-                near[k].wait_send()
-                far[k].wait_send()
+        store_att = pltpu.make_async_copy(att, attended, out_sem.at[1])
+        store_att.start()
+        if comm:
+            for part in near + far:
+                part.wait_send()
 
             @pl.when(hop_out)
             def _():
@@ -394,9 +397,38 @@
                         state_copy(sweep, chunk).wait_send()
 
         store_state.wait()
-        store_mixed.wait()
+        store_att.wait()
 
     return kernel
+
+
+TILE = 256
+
+
+def finish_kernel(tokens, state, wo, attended, mixed, new_state, vout, sem):
+    store_state = pltpu.make_async_copy(state, new_state, sem.at[0])
+    store_state.start()
+    stores = []
+    for n in range(D // TILE):
+        cols = pl.ds(n * TILE, TILE)
+        vout[:, cols] = (tokens[:, cols].astype(F32) + dot(attended[...], wo[:, cols])).astype(BF16)
+        stores.append(pltpu.make_async_copy(vout.at[:, cols], mixed.at[:, cols], sem.at[1 + n]))
+        stores[-1].start()
+    store_state.wait()
+    for store in stores:
+        store.wait()
+
+
+def make_finish():
+    return pl.pallas_call(
+        finish_kernel,
+        name="finish",
+        out_shape=(jax.ShapeDtypeStruct((SEG, D), BF16), jax.ShapeDtypeStruct((SEG, D), BF16)),
+        in_specs=[pl.BlockSpec(memory_space=pltpu.VMEM)] * 4,
+        out_specs=(pl.BlockSpec(memory_space=pl.ANY),) * 2,
+        scratch_shapes=[pltpu.VMEM((SEG, D), BF16), pltpu.SemaphoreType.DMA((1 + D // TILE,))],
+        compiler_params=pltpu.CompilerParams(vmem_limit_bytes=16 << 20),
+    )
 
 
 def make_call(count, comm):
@@ -407,21 +439,21 @@
         make_kernel(count, comm),
         name="layer",
         out_shape=(jax.ShapeDtypeStruct((SEG, D), BF16), jax.ShapeDtypeStruct((SEG, D), BF16)),
-        in_specs=[pl.BlockSpec(memory_space=pl.ANY)] * 10
+        in_specs=[pl.BlockSpec(memory_space=pl.ANY)] * 9
         + [pl.BlockSpec(memory_space=pltpu.VMEM)]
         + [pl.BlockSpec(memory_space=pltpu.SMEM)] * 2,
         out_specs=(pl.BlockSpec(memory_space=pl.ANY),) * 2,
         scratch_shapes=[
             pltpu.VMEM((5 * RET, BLK, D), BF16), seg, pltpu.VMEM((RET, BLK, D), BF16),
-            square, square, square, square, square, wide, wide,
+            square, square, square, square, wide, wide,
             seg, seg, seg, seg, pltpu.VMEM((SEG, 2 * D), BF16), seg, seg,
             seg, seg, pltpu.VMEM((ITERS, SEG, D), BF16), pltpu.VMEM((ITERS, SEG, D), BF16), seg, seg, seg,
             pltpu.VMEM((SEG, 2 * D), F32), pltpu.VMEM((SEG, D), F32),
             pltpu.SemaphoreType.DMA((12,)), pltpu.SemaphoreType.DMA((2,)),
-            pltpu.SemaphoreType.DMA((12 + ITERS * CHUNKS,)), pltpu.SemaphoreType.DMA((12 + ITERS * CHUNKS,)),
+            pltpu.SemaphoreType.DMA((14 + ITERS * CHUNKS,)), pltpu.SemaphoreType.DMA((14 + ITERS * CHUNKS,)),
         ],
         compiler_params=pltpu.CompilerParams(
-            collective_id=0 if comm else None, has_side_effects=True, vmem_limit_bytes=62 << 20
+            collective_id=0 if comm else None, has_side_effects=True, vmem_limit_bytes=54 << 20
         ),
     )
 
@@ -431,10 +463,11 @@
 
     def per_device(tokens, init_state, w_query, w_key, w_value, w_out, w_query_state, w_cand_gate,
                    w_state_kv, gate_bias, mixing, retrieval):
-        return make_call(count, True)(
-            tokens.reshape(RET, BLK, D), tokens, init_state, w_query, w_key, w_value, w_out, w_query_state, w_cand_gate,
+        attended, state = make_call(count, True)(
+            tokens.reshape(RET, BLK, D), tokens, init_state, w_query, w_key, w_value, w_query_state, w_cand_gate,
             w_state_kv, gate_bias.reshape(1, -1), mixing, retrieval,
         )
+        return make_finish()(tokens, state, w_out, attended)
 
     return jax.shard_map(
         per_device,

time: 74.5 us -> 71.3 us (0.957)
  Pallas kernels: 70.4 us -> 67.8 us
  local copies, waits for them, and re-layouts: 3.32 us -> 2.45 us
    pallas_call x1, Pallas kernels: 70.4 us -> 65.7 us  [per_device(): make_call(count, True)]
    pallas_call x0 -> x1, Pallas kernels: none -> 2.13 us  [per_device(): return make_finish()(tokens, state, w_out, attended)]
    unnamed x4 -> x8, local copies, waits for them, and re-layouts: 3.32 us -> 2.45 us
where the time goes in v3:
time: 71.3 us; the launch traced here: 71.1 us
  Pallas kernels  67.8 us (95%)
  local copies, waits for them, and re-layouts  2.45 us (3%)
  between operations  0.84 us (1%)
    pallas_call x1, Pallas kernels, per_device(): make_call(count, True)  65.7 us
    unnamed x8, local copies, waits for them, and re-layouts  2.45 us
    pallas_call x1, Pallas kernels, per_device(): return make_finish()(tokens, state, w_out, attended)  2.13 us

profile of v3, /device:TPU:97, one launch (start us, length us, event | category | flops | bytes accessed | tf_op | source)
XLA Modules:
  0.0 71.1 jit_solution(8242425428156246844)
XLA Ops:
  0.6 0.0 copy-start
  0.6 0.0 copy-start.1
  0.7 65.7 %layer.1 = (bf16[512,1024]{1,0:T(8,128)(2,1)}, bf16[512,1024]{1,0:T(8,128)(2,1)}) custom-call(bf16[8,64,1024]{2,1,0:T(8,128)(2,1)} %bitcast.2, bf16[512,1024]{1,0:T(8,128)(2,1)} %tokens.1, bf16[512,1024]{1,0:T(8,128)(2,1)} %init.1, bf16[1024,1024]{1,0:T(8,128)(2,1)} %wq.1, bf16[1024,1024]{1,0:T(8,128)(2,1)} %wk.1, bf16[1024,1024]{1,0:T(8,128)(2,1)} %wv.1, ...), custom_call_target="tpu_custom_call" | custom-call | tf_op jit(solution)/shard_map/layer/pallas_call | solution.py:466
  66.3 0.0 copy-done
  66.3 0.0 copy-done.1
  66.4 0.0 copy-start.2
  66.4 1.2 %copy-done.2 = bf16[512,1024]{1,0:T(8,128)(2,1)S(1)} copy-done((bf16[512,1024]{1,0:T(8,128)(2,1)S(1)}, bf16[512,1024]{1,0:T(8,128)(2,1)}, u32[]{:S(2)}) %copy-start.2) | copy-done | bytes 1048600
  67.6 0.0 copy-start.3
  67.6 1.2 %copy-done.3 = bf16[512,1024]{1,0:T(8,128)(2,1)S(1)} copy-done((bf16[512,1024]{1,0:T(8,128)(2,1)S(1)}, bf16[512,1024]{1,0:T(8,128)(2,1)}, u32[]{:S(2)}) %copy-start.3) | copy-done | bytes 1048600
  68.8 2.1 %finish.1 = (bf16[512,1024]{1,0:T(8,128)(2,1)}, bf16[512,1024]{1,0:T(8,128)(2,1)}) custom-call(bf16[512,1024]{1,0:T(8,128)(2,1)S(1)} %copy-done, bf16[512,1024]{1,0:T(8,128)(2,1)S(1)} %copy-done.3, bf16[1024,1024]{1,0:T(8,128)(2,1)S(1)} %copy-done.1, bf16[512,1024]{1,0:T(8,128)(2,1)S(1)} %copy-done.2), custom_call_target="tpu_custom_call" | custom-call | tf_op jit(solution)/shard_map/finish/pallas_call | solution.py:470
Async XLA Ops:
  0.6 65.7 %copy-start = (bf16[512,1024]{1,0:T(8,128)(2,1)S(1)}, bf16[512,1024]{1,0:T(8,128)(2,1)}, u32[]{:S(2)}) copy-start(bf16[512,1024]{1,0:T(8,128)(2,1)} %tokens.1) | copy-start | bytes 3145732
  0.6 65.7 %copy-start.1 = (bf16[1024,1024]{1,0:T(8,128)(2,1)S(1)}, bf16[1024,1024]{1,0:T(8,128)(2,1)}, u32[]{:S(2)}) copy-start(bf16[1024,1024]{1,0:T(8,128)(2,1)} %wo.1) | copy-start | bytes 6291460
  66.4 1.2 %copy-start.2 = (bf16[512,1024]{1,0:T(8,128)(2,1)S(1)}, bf16[512,1024]{1,0:T(8,128)(2,1)}, u32[]{:S(2)}) copy-start(bf16[512,1024]{1,0:T(8,128)(2,1)} %get-tuple-element.5.attended) | copy-start | bytes 3145732
  67.6 1.2 %copy-start.3 = (bf16[512,1024]{1,0:T(8,128)(2,1)S(1)}, bf16[512,1024]{1,0:T(8,128)(2,1)}, u32[]{:S(2)}) copy-start(bf16[512,1024]{1,0:T(8,128)(2,1)} %get-tuple-element.4.state) | copy-start | bytes 3145732

commit v4 on v3

--- a/solution.py
+++ b/solution.py
@@ -264,6 +264,8 @@
                     guess[rows] = (
                         mixing[sweep - 1, 0] * moved + mixing[sweep - 1, 1] * held + mixing[sweep - 1, 2] * older
                     ).astype(BF16)
+                if sweep == ITERS:
+                    state_memory(chunk)
                 project(query.at[rows], source.at[rows], vqs, D)
                 if sweep < ITERS and comm:
                     @pl.when(jnp.logical_and(chunk > 0, me < count - 1))
@@ -291,6 +293,25 @@
                 def _():
                     state_copy(sweep, CHUNKS - 1).start()
 
+        def state_memory(chunk):
+            rows = rows_of(chunk)
+
+            @pl.when(chunk == 0)
+            def _():
+                loads["wskv"].wait()
+
+            project(skv.at[rows], guess.at[rows], vskv, 2 * D)
+
+            def state_part(part, carry):
+                here = rows_of(part)
+                partial_attention(
+                    qtok.at[here], skv.at[rows, pl.ds(0, D)], skv.at[rows, pl.ds(D, D)],
+                    acc.at[here], peak.at[here], None, False, None,
+                )
+                return carry
+
+            lax.fori_loop(0, CHUNKS, state_part, 0)
+
         def local_attention(chunk, heads):
             rows = slice(chunk * ROWS, (chunk + 1) * ROWS)
             width = (chunk + 1) * ROWS
@@ -329,23 +350,8 @@
             exchange(range(1), (0,))
         forward_state(2)
         store_state = pltpu.make_async_copy(final, new_state, out_sem.at[0])
-        loads["wskv"].wait()
-        project(skv, guess, vskv, 2 * D)
-        store_state.start()
         if comm:
             relay_arrived(0)
-
-        def state_part(chunk, carry):
-            rows = rows_of(chunk)
-            partial_attention(
-                qtok.at[rows], skv.at[:, pl.ds(0, D)], skv.at[:, pl.ds(D, D)],
-                acc.at[rows], peak.at[rows], None, False, None,
-            )
-            return carry
-
-        lax.fori_loop(0, CHUNKS, state_part, 0)
-
-        if comm:
             exchange(range(1, 4), (1,))
             for part in near + far:
                 part.wait_recv()
@@ -357,6 +363,7 @@
             xmem[e * BLK : (e + 1) * BLK] = buf[RET + block]
             usable = jnp.where(block // 8 + 1 <= me, 1, 0)
             open_column = jnp.where(column == e, usable, open_column)
+        store_state.start()
         project(mkey, xmem, vk, D)
         project(mvalue, xmem, vv, D)
 
@@ -405,29 +412,50 @@
 TILE = 256
 
 
-def finish_kernel(tokens, state, wo, attended, mixed, new_state, vout, sem):
-    store_state = pltpu.make_async_copy(state, new_state, sem.at[0])
-    store_state.start()
-    stores = []
-    for n in range(D // TILE):
-        cols = pl.ds(n * TILE, TILE)
-        vout[:, cols] = (tokens[:, cols].astype(F32) + dot(attended[...], wo[:, cols])).astype(BF16)
-        stores.append(pltpu.make_async_copy(vout.at[:, cols], mixed.at[:, cols], sem.at[1 + n]))
-        stores[-1].start()
+def finish_kernel(tokens, state, wo, attended, mixed, new_state, vtok, vstate, vo, vatt, vout, sem):
+    tiles = D // TILE
+
+    def tile(n):
+        return pl.ds(n * TILE, TILE)
+
+    load_att = pltpu.make_async_copy(attended, vatt, sem.at[0])
+    load_wo = [pltpu.make_async_copy(wo.at[:, tile(n)], vo.at[:, tile(n)], sem.at[1 + n]) for n in range(tiles)]
+    load_tok = pltpu.make_async_copy(tokens, vtok, sem.at[1 + tiles])
+    load_state = pltpu.make_async_copy(state, vstate, sem.at[2 + tiles])
+    store_state = pltpu.make_async_copy(vstate, new_state, sem.at[3 + tiles])
+    store = [pltpu.make_async_copy(vout.at[:, tile(n)], mixed.at[:, tile(n)], sem.at[4 + tiles + n]) for n in range(tiles)]
+    load_att.start()
+    load_wo[0].start()
+    load_tok.start()
+    for n in range(1, tiles):
+        load_wo[n].start()
+    load_state.start()
+    load_att.wait()
+    for n in range(tiles):
+        load_wo[n].wait()
+        product = dot(vatt[...], vo[:, tile(n)])
+        if n == 0:
+            load_tok.wait()
+        vout[:, tile(n)] = (vtok[:, tile(n)].astype(F32) + product).astype(BF16)
+        store[n].start()
+        if n == 0:
+            load_state.wait()
+            store_state.start()
     store_state.wait()
-    for store in stores:
-        store.wait()
+    for n in range(tiles):
+        store[n].wait()
 
 
 def make_finish():
+    seg = pltpu.VMEM((SEG, D), BF16)
     return pl.pallas_call(
         finish_kernel,
         name="finish",
         out_shape=(jax.ShapeDtypeStruct((SEG, D), BF16), jax.ShapeDtypeStruct((SEG, D), BF16)),
-        in_specs=[pl.BlockSpec(memory_space=pltpu.VMEM)] * 4,
+        in_specs=[pl.BlockSpec(memory_space=pl.ANY)] * 4,
         out_specs=(pl.BlockSpec(memory_space=pl.ANY),) * 2,
-        scratch_shapes=[pltpu.VMEM((SEG, D), BF16), pltpu.SemaphoreType.DMA((1 + D // TILE,))],
-        compiler_params=pltpu.CompilerParams(vmem_limit_bytes=16 << 20),
+        scratch_shapes=[seg, seg, pltpu.VMEM((D, D), BF16), seg, seg, pltpu.SemaphoreType.DMA((4 + 2 * (D // TILE),))],
+        compiler_params=pltpu.CompilerParams(vmem_limit_bytes=62 << 20),
     )
 
 
@@ -453,7 +481,7 @@
             pltpu.SemaphoreType.DMA((14 + ITERS * CHUNKS,)), pltpu.SemaphoreType.DMA((14 + ITERS * CHUNKS,)),
         ],
         compiler_params=pltpu.CompilerParams(
-            collective_id=0 if comm else None, has_side_effects=True, vmem_limit_bytes=54 << 20
+            collective_id=0 if comm else None, has_side_effects=True, vmem_limit_bytes=62 << 20
         ),
     )
 

time: 71.3 us -> 70.2 us (0.985)
  local copies, waits for them, and re-layouts: 2.45 us -> 0 us
  Pallas kernels: 67.8 us -> 69.3 us
    pallas_call x1, Pallas kernels: 2.13 us -> 5.41 us  [per_device(): return make_finish()(tokens, state, w_out, attended)]
    unnamed x8 -> x0, local copies, waits for them, and re-layouts: 2.45 us -> none
    pallas_call x1, Pallas kernels: 65.7 us -> 63.9 us  [per_device(): make_call(count, True)]
where the time goes in v4:
time: 70.2 us; the launch traced here: 70.1 us
  Pallas kernels  69.3 us (99%)
  between operations  0.8 us (1%)
    pallas_call x1, Pallas kernels, per_device(): make_call(count, True)  63.9 us
    pallas_call x1, Pallas kernels, per_device(): return make_finish()(tokens, state, w_out, attended)  5.41 us

profile of v4, /device:TPU:97, one launch (start us, length us, event | category | flops | bytes accessed | tf_op | source)
XLA Modules:
  0.0 70.1 jit_solution(12460547594324856545)
XLA Ops:
  0.6 63.9 %layer.1 = (bf16[512,1024]{1,0:T(8,128)(2,1)}, bf16[512,1024]{1,0:T(8,128)(2,1)}) custom-call(bf16[8,64,1024]{2,1,0:T(8,128)(2,1)} %bitcast.2, bf16[512,1024]{1,0:T(8,128)(2,1)} %tokens.1, bf16[512,1024]{1,0:T(8,128)(2,1)} %init.1, bf16[1024,1024]{1,0:T(8,128)(2,1)} %wq.1, bf16[1024,1024]{1,0:T(8,128)(2,1)} %wk.1, bf16[1024,1024]{1,0:T(8,128)(2,1)} %wv.1, ...), custom_call_target="tpu_custom_call" | custom-call | tf_op jit(solution)/shard_map/layer/pallas_call | solution.py:494
  64.5 5.4 %finish.1 = (bf16[512,1024]{1,0:T(8,128)(2,1)}, bf16[512,1024]{1,0:T(8,128)(2,1)}) custom-call(bf16[512,1024]{1,0:T(8,128)(2,1)} %tokens.1, bf16[512,1024]{1,0:T(8,128)(2,1)} %get-tuple-element.4.state, bf16[1024,1024]{1,0:T(8,128)(2,1)} %wo.1, bf16[512,1024]{1,0:T(8,128)(2,1)} %get-tuple-element.5.attended), custom_call_target="tpu_custom_call" | custom-call | tf_op jit(solution)/shard_map/finish/pallas_call | solution.py:498

commit v5 on v3

--- a/solution.py
+++ b/solution.py
@@ -264,6 +264,8 @@
                     guess[rows] = (
                         mixing[sweep - 1, 0] * moved + mixing[sweep - 1, 1] * held + mixing[sweep - 1, 2] * older
                     ).astype(BF16)
+                if sweep == ITERS:
+                    state_memory(chunk)
                 project(query.at[rows], source.at[rows], vqs, D)
                 if sweep < ITERS and comm:
                     @pl.when(jnp.logical_and(chunk > 0, me < count - 1))
@@ -291,6 +293,25 @@
                 def _():
                     state_copy(sweep, CHUNKS - 1).start()
 
+        def state_memory(chunk):
+            rows = rows_of(chunk)
+
+            @pl.when(chunk == 0)
+            def _():
+                loads["wskv"].wait()
+
+            project(skv.at[rows], guess.at[rows], vskv, 2 * D)
+
+            def state_part(part, carry):
+                here = rows_of(part)
+                partial_attention(
+                    qtok.at[here], skv.at[rows, pl.ds(0, D)], skv.at[rows, pl.ds(D, D)],
+                    acc.at[here], peak.at[here], None, False, None,
+                )
+                return carry
+
+            lax.fori_loop(0, CHUNKS, state_part, 0)
+
         def local_attention(chunk, heads):
             rows = slice(chunk * ROWS, (chunk + 1) * ROWS)
             width = (chunk + 1) * ROWS
@@ -329,23 +350,8 @@
             exchange(range(1), (0,))
         forward_state(2)
         store_state = pltpu.make_async_copy(final, new_state, out_sem.at[0])
-        loads["wskv"].wait()
-        project(skv, guess, vskv, 2 * D)
-        store_state.start()
         if comm:
             relay_arrived(0)
-
-        def state_part(chunk, carry):
-            rows = rows_of(chunk)
-            partial_attention(
-                qtok.at[rows], skv.at[:, pl.ds(0, D)], skv.at[:, pl.ds(D, D)],
-                acc.at[rows], peak.at[rows], None, False, None,
-            )
-            return carry
-
-        lax.fori_loop(0, CHUNKS, state_part, 0)
-
-        if comm:
             exchange(range(1, 4), (1,))
             for part in near + far:
                 part.wait_recv()
@@ -357,6 +363,7 @@
             xmem[e * BLK : (e + 1) * BLK] = buf[RET + block]
             usable = jnp.where(block // 8 + 1 <= me, 1, 0)
             open_column = jnp.where(column == e, usable, open_column)
+        store_state.start()
         project(mkey, xmem, vk, D)
         project(mvalue, xmem, vv, D)
 

time: 71.3 us -> 69.5 us (0.975)
  Pallas kernels: 67.8 us -> 66 us
    pallas_call x1, Pallas kernels: 65.7 us -> 63.9 us  [per_device(): make_call(count, True)]
where the time goes in v5:
time: 69.5 us; the launch traced here: 69.3 us
  Pallas kernels  66 us (95%)
  local copies, waits for them, and re-layouts  2.45 us (4%)
  between operations  0.84 us (1%)
    pallas_call x1, Pallas kernels, per_device(): make_call(count, True)  63.9 us
    unnamed x8, local copies, waits for them, and re-layouts  2.45 us
    pallas_call x1, Pallas kernels, per_device(): return make_finish()(tokens, state, w_out, attended)  2.13 us

profile of v5, /device:TPU:97, one launch (start us, length us, event | category | flops | bytes accessed | tf_op | source)
XLA Modules:
  0.0 69.3 jit_solution(5488800095896751390)
XLA Ops:
  0.6 0.0 copy-start
  0.6 0.0 copy-start.1
  0.7 63.9 %layer.1 = (bf16[512,1024]{1,0:T(8,128)(2,1)}, bf16[512,1024]{1,0:T(8,128)(2,1)}) custom-call(bf16[8,64,1024]{2,1,0:T(8,128)(2,1)} %bitcast.2, bf16[512,1024]{1,0:T(8,128)(2,1)} %tokens.1, bf16[512,1024]{1,0:T(8,128)(2,1)} %init.1, bf16[1024,1024]{1,0:T(8,128)(2,1)} %wq.1, bf16[1024,1024]{1,0:T(8,128)(2,1)} %wk.1, bf16[1024,1024]{1,0:T(8,128)(2,1)} %wv.1, ...), custom_call_target="tpu_custom_call" | custom-call | tf_op jit(solution)/shard_map/layer/pallas_call | solution.py:473
  64.5 0.0 copy-done
  64.5 0.0 copy-done.1
  64.5 0.0 copy-start.2
  64.5 1.2 %copy-done.2 = bf16[512,1024]{1,0:T(8,128)(2,1)S(1)} copy-done((bf16[512,1024]{1,0:T(8,128)(2,1)S(1)}, bf16[512,1024]{1,0:T(8,128)(2,1)}, u32[]{:S(2)}) %copy-start.2) | copy-done | bytes 1048600
  65.8 0.0 copy-start.3
  65.8 1.2 %copy-done.3 = bf16[512,1024]{1,0:T(8,128)(2,1)S(1)} copy-done((bf16[512,1024]{1,0:T(8,128)(2,1)S(1)}, bf16[512,1024]{1,0:T(8,128)(2,1)}, u32[]{:S(2)}) %copy-start.3) | copy-done | bytes 1048600
  67.0 2.1 %finish.1 = (bf16[512,1024]{1,0:T(8,128)(2,1)}, bf16[512,1024]{1,0:T(8,128)(2,1)}) custom-call(bf16[512,1024]{1,0:T(8,128)(2,1)S(1)} %copy-done, bf16[512,1024]{1,0:T(8,128)(2,1)S(1)} %copy-done.3, bf16[1024,1024]{1,0:T(8,128)(2,1)S(1)} %copy-done.1, bf16[512,1024]{1,0:T(8,128)(2,1)S(1)} %copy-done.2), custom_call_target="tpu_custom_call" | custom-call | tf_op jit(solution)/shard_map/finish/pallas_call | solution.py:477
Async XLA Ops:
  0.6 63.9 %copy-start = (bf16[512,1024]{1,0:T(8,128)(2,1)S(1)}, bf16[512,1024]{1,0:T(8,128)(2,1)}, u32[]{:S(2)}) copy-start(bf16[512,1024]{1,0:T(8,128)(2,1)} %tokens.1) | copy-start | bytes 3145732
  0.6 63.9 %copy-start.1 = (bf16[1024,1024]{1,0:T(8,128)(2,1)S(1)}, bf16[1024,1024]{1,0:T(8,128)(2,1)}, u32[]{:S(2)}) copy-start(bf16[1024,1024]{1,0:T(8,128)(2,1)} %wo.1) | copy-start | bytes 6291460
  64.5 1.2 %copy-start.2 = (bf16[512,1024]{1,0:T(8,128)(2,1)S(1)}, bf16[512,1024]{1,0:T(8,128)(2,1)}, u32[]{:S(2)}) copy-start(bf16[512,1024]{1,0:T(8,128)(2,1)} %get-tuple-element.5.attended) | copy-start | bytes 3145732
  65.8 1.2 %copy-start.3 = (bf16[512,1024]{1,0:T(8,128)(2,1)S(1)}, bf16[512,1024]{1,0:T(8,128)(2,1)}, u32[]{:S(2)}) copy-start(bf16[512,1024]{1,0:T(8,128)(2,1)} %get-tuple-element.4.state) | copy-start | bytes 3145732
